TPU v7x, 128 devices: a whole 4x4x4 slice. The times are simulated.
128 devices in a mesh: vert: 64 (over z, y_hi, x, core), row: 2 (over y_lo).
Axes of the slice: x: 4, y: 4 (y_hi: 2, y_lo: 2; y = y_hi * 2 + y_lo), z: 4, core: 2. Of those that a mesh axis runs over, the one named last changes fastest.
Arguments:
- features: float32 [524288, 256], P(('vert', 'row')), may hold values from -6 to 6
- w_self: float32 [256, 256], replicated, may hold values from -0.375 to 0.375
- w_neigh: float32 [256, 256], replicated, may hold values from -0.75 to 0.75
- bias: float32 [256], replicated, may hold values from -3 to 3
- w_head: float32 [256], replicated, may hold values from -0.75 to 0.75
- tile_weights: float32 [16384, 128, 128], P(('vert', 'row')), may hold values from 0.01 to 1
- tile_dst: int32 [16384], P(('vert', 'row')), may hold values from 0 to 31
- tile_src: int32 [16384], P(('vert', 'row')), may hold values from 0 to 167
- tile_count: int32 [128], P(('vert', 'row')), may hold values from 16 to 128, as said below
- hub_block: int32 [128], P(('vert', 'row')), may hold values from 0 to 31
- send_rows: int32 [128, 128, 8], P(('vert', 'row')), may hold values from 0 to 4095
- send_count: int32 [128, 128], P(('vert', 'row')), may hold values from 1 to 8, as said below
- labels: int32 [524288], P(('vert', 'row')), may hold values from 0 to 1
Outputs:
- grad_self: float32 [256, 256], replicated
- grad_neigh: float32 [256, 256], replicated
- grad_bias: float32 [256], replicated
- grad_head: float32 [256], replicated
Inputs may be any that keep to these rules, and one draw needn't show every extreme that they name: Tile t of a device is used when t < its tile_count; some device uses all 128 tiles and some 128 // 8. `send_count`: each sending device fills all 8 slots for at least one receiving device.
All inputs are finite; a program needn't handle non-finite values.
Results may differ from a plain program's by a relative error of at most 0.0003.
Values sent between devices are 32-bit elements; how exact they have to be, the bound alone decides.
A program may use at most 128 MiB of HBM per device.

v0:
```python
import math
import jax
import jax.numpy as jnp
from jax import lax
from jax.sharding import PartitionSpec as P

FULL_PRECISION = lax.Precision.HIGHEST


def on_device(
    features,
    w_self,
    w_neigh,
    bias,
    w_head,
    tile_weights,
    tile_dst,
    tile_src,
    tile_count,
    hub_block,
    send_rows,
    send_count,
    labels,
):
    tile_size = tile_weights.shape[1]
    tile_total = tile_weights.shape[0]
    feature_width = features.shape[1]
    block_count = features.shape[0] // tile_size
    slot_count = send_rows.shape[2]
    own_blocks = features.reshape(block_count, tile_size, feature_width)
    hub_local = lax.dynamic_slice_in_dim(own_blocks, hub_block[0], 1, 0)
    hub_blocks = lax.all_gather(hub_local, ("vert", "row"), axis=0, tiled=True)
    outgoing = features[send_rows[0]]
    slot_index = jnp.arange(slot_count, dtype=jnp.int32)
    alive = slot_index[None, :] < send_count[0][:, None]
    outgoing = jnp.where(alive[:, :, None], outgoing, jnp.zeros_like(outgoing))
    incoming = lax.all_to_all(outgoing, ("vert", "row"), split_axis=0, concat_axis=0, tiled=True)
    source_table = jnp.concatenate(
        [own_blocks, incoming.reshape(-1, tile_size, feature_width), hub_blocks], 0
    )
    active = jnp.arange(tile_total, dtype=jnp.int32) < tile_count[0]
    picked = source_table[tile_src]
    contrib = jnp.einsum("tij,tjf->tif", tile_weights, picked, precision=FULL_PRECISION)
    block_ids = jnp.arange(block_count, dtype=jnp.int32)
    selector = ((tile_dst[None, :] == block_ids[:, None]) & active[None, :]).astype(features.dtype)
    summed = jnp.einsum("bt,tif->bif", selector, contrib, precision=FULL_PRECISION)
    weight_sum = jnp.einsum(
        "bt,ti->bi", selector, jnp.sum(tile_weights, axis=2), precision=FULL_PRECISION
    )
    neigh_mean = ((own_blocks + summed) / (1.0 + weight_sum)[:, :, None]).reshape(-1, feature_width)
    pre_act = (
        jnp.dot(features, w_self, precision=FULL_PRECISION)
        + jnp.dot(neigh_mean, w_neigh, precision=FULL_PRECISION)
        + bias[None, :]
    )
    sigmoid_pre = jax.nn.sigmoid(pre_act)
    hidden = pre_act * sigmoid_pre
    head_score = jnp.dot(hidden, w_head, precision=FULL_PRECISION)
    target = 2.0 * labels.astype(features.dtype) - 1.0
    vertex_total = features.shape[0] * lax.axis_size(("vert", "row"))
    loss_scale = 1.0 / math.sqrt(vertex_total)
    dscore = (head_score - target) * loss_scale
    dpre = dscore[:, None] * w_head[None, :] * (sigmoid_pre * (1.0 + pre_act * (1.0 - sigmoid_pre)))
    local_self = jnp.dot(features.T, dpre, precision=FULL_PRECISION)
    local_neigh = jnp.dot(neigh_mean.T, dpre, precision=FULL_PRECISION)
    local_bias = jnp.sum(dpre, axis=0)
    local_head = jnp.dot(hidden.T, dscore, precision=FULL_PRECISION)
    grad_self, grad_neigh, grad_bias, grad_head = lax.psum(
        (local_self, local_neigh, local_bias, local_head), ("vert", "row")
    )
    return (grad_self, grad_neigh, grad_bias, grad_head)


def solution(mesh):
    in_specs = (
        P(("vert", "row"), None),
        P(),
        P(),
        P(),
        P(),
        P(("vert", "row"), None, None),
        P(("vert", "row")),
        P(("vert", "row")),
        P(("vert", "row")),
        P(("vert", "row")),
        P(("vert", "row"), None, None),
        P(("vert", "row"), None),
        P(("vert", "row")),
    )
    out_specs = (P(), P(), P(), P())
    return jax.shard_map(
        on_device, mesh=mesh, in_specs=in_specs, out_specs=out_specs, check_vma=False
    )
```

profile of v0, /device:TPU:1, one launch (start us, length us, event | category | flops | bytes accessed | tf_op | source)
XLA Modules:
  0.0 630.4 jit_solution(8257241849353653896)
XLA Ops:
  7.2 0.0 copy-start
  7.2 0.0 all-gather.2.cloned.1.call-start
  7.9 1.6 constant_dynamic-slice_fusion
  9.5 0.0 all-gather.2.cloned.1.call-update
  9.5 0.7 compare_select_fusion
  10.2 0.1 copy.24
  10.3 0.1 reshape.83
  10.4 0.0 copy-start.10
  10.4 5.7 gather_fusion
  16.1 0.0 copy-done.10
  16.1 0.1 iota_compare_fusion
  16.2 1.2 bitcast_select_fusion
  17.4 11.5 %all-to-all-start = ((f32[128,8,256]{2,1,0:T(8,128)}), f32[128,8,256]{2,1,0:T(8,128)S(1)}, u32[]{:S(2)}, u32[]{:S(2)}) async-start(f32[128,8,256]{2,1,0:T(8,128)} %bitcast_select_fusion), calls=%async_computation | async-start | bytes 2097152 | tf_op jit(solution)/shard_map/all_to_all | solution.py:37
  28.9 0.0 all-reduce.4.cloned.1.call-start
  29.6 0.0 copy-start.7
  29.6 0.0 copy-start.11
  29.6 5.6 reduce_sum.18
  35.3 0.1 convolution_add_fusion.1
  35.4 0.1 copy.28
  35.6 7.6 %fusion.21 = f32[4096,256]{1,0:T(8,128)} fusion(f32[4096,256]{1,0:T(8,128)} %param.13, f32[256,256]{1,0:T(8,128)S(1)} %copy-done), kind=kOutput, calls=%fused_computation.41 | convolution fusion | flops 3221225472 | bytes 8650752 | tf_op jit(solution)/shard_map/dot_general | solution.py:52
  43.2 8.0 %all-to-all-done = f32[128,8,256]{2,1,0:T(8,128)S(1)} async-done(((f32[128,8,256]{2,1,0:T(8,128)}), f32[128,8,256]{2,1,0:T(8,128)S(1)}, u32[]{:S(2)}, u32[]{:S(2)}) %all-to-all-start) | async-done | bytes 1048608 | tf_op jit(solution)/shard_map/all_to_all | solution.py:37
  51.2 294.8 %all-gather.2.cloned.1.call-done = f32[128,128,256]{2,1,0:T(8,128)} async-done(((f32[1,128,256]{2,1,0:T(8,128)}), f32[128,128,256]{2,1,0:T(8,128)}) %all-gather.2.cloned.1.call-update) | async-done | bytes 16777232 | tf_op jit(solution)/shard_map/all_gather | solution.py:32
  346.0 15.9 %pad_maximum_fusion = f32[168,128,256]{2,1,0:T(8,128)} fusion(f32[128,128,256]{2,1,0:T(8,128)} %all-gather.2.cloned.1.call-done, f32[8,128,256]{2,1,0:T(8,128)S(1)} %bitcast.58, f32[32,128,256]{2,1,0:T(8,128)} %bitcast.54), kind=kLoop, calls=%fused_computation.2 | loop fusion | flops 11010048 | bytes 44040192 | tf_op jit(solution)/shard_map/concatenate | solution.py:38
  362.0 17.3 %gather_fusion.1 = f32[128,128,256]{2,1,0:T(8,128)} fusion(f32[168,128,256]{2,1,0:T(8,128)} %pad_maximum_fusion, s32[1024]{0:T(1024)S(1)} %pad_clamp_fusion), kind=kCustom, calls=%fused_computation.1 | custom fusion | bytes 33554944 | tf_op jit(solution)/shard_map/gather | solution.py:42
  379.3 34.3 %convolution_bitcast_fusion = f32[128,128,256]{1,2,0:T(8,128)} fusion(f32[128,128,256]{2,1,0:T(8,128)} %gather_fusion.1, f32[128,128,128]{2,1,0:T(8,128)} %param.18), kind=kOutput, calls=%fused_computation.3 | convolution fusion | flops 6442450944 | bytes 41943040 | tf_op jit(solution)/shard_map/tij,tjf->tif/dot_general | solution.py:43
  413.6 17.7 %copy.26 = f32[128,128,256]{2,0,1:T(8,128)} copy(f32[128,128,256]{1,2,0:T(8,128)} %convolution_bitcast_fusion) | data formatting | bytes 33554432 | tf_op jit(solution)/shard_map/tij,tjf->tif/dot_general | solution.py:43
  431.2 13.7 %fusion.4 = f32[32,128,256]{2,0,1:T(8,128)S(1)} fusion(f32[32,128,256]{2,1,0:T(8,128)} %bitcast.55, f32[128,128,256]{2,0,1:T(8,128)} %copy.26, f32[32,128]{0,1:T(8,128)S(1)} %copy.28, s32[128]{0:T(128)S(1)} %copy-done.7, pred[128]{0:T(512)(128)(4,1)S(1)} %iota_compare_fusion.2), kind=kOutput, calls=%fused_computation.12 | convolution fusion | flops 1612718080 | bytes 25182848 | tf_op jit(solution)/shard_map/bt,tif->bif/dot_general | solution.py:46
  445.0 0.0 copy-start.5
  445.0 0.0 copy-start.8
  445.0 2.4 copy.29
  447.4 0.0 copy-done.4
  447.4 0.0 copy-done.5
  447.4 0.0 copy-done.8
  447.5 0.0 copy-start.9
  447.5 3.4 fusion
  450.9 0.0 copy-start.6
  450.9 4.4 fusion.5
  455.4 2.4 fusion.20
  457.9 0.0 copy-start.2
  457.9 7.5 %fusion.22 = f32[256,256]{1,0:T(8,128)} fusion(f32[4096,256]{1,0:T(8,128)S(1)} %bitcast.57, f32[4096,256]{1,0:T(8,128)S(1)} %get-tuple-element.21), kind=kOutput, calls=%fused_computation.42 | convolution fusion | flops 3221225472 | bytes 8650752 | tf_op jit(solution)/shard_map/dot_general | solution.py:65
  465.4 7.7 %convolution_bitcast_fusion.1 = f32[256,256]{0,1:T(8,128)} fusion(f32[4096,256]{1,0:T(8,128)S(1)} %get-tuple-element.21, f32[4096,256]{1,0:T(8,128)S(1)} %copy-done.2), kind=kOutput, calls=%fused_computation.20 | convolution fusion | flops 3221225472 | bytes 8650752 | tf_op jit(solution)/shard_map/dot_general | solution.py:64
  473.0 0.0 all-reduce.4.cloned.1.call-update
  473.1 0.0 copy-start.1
  473.1 5.2 fusion.7
  478.2 67.7 %all-reduce = (f32[256]{0:T(256)}, f32[256]{0:T(256)}) all-reduce(f32[256]{0:T(256)S(1)} %get-tuple-element.20, f32[256]{0:T(256)S(1)} %bitcast.62), channel_id=1, replica_groups=mesh['vert'=64,'row'=2] {'vert','row'}, use_global_device_ids=true, to_apply=%region_4.5 | all-reduce | flops 512 | bytes 4096 | tf_op jit(solution)/shard_map/psum | solution.py:68
  545.9 74.0 %all-reduce.4.cloned.1.call-done = (f32[256,256]{0,1:T(8,128)}, f32[256,256]{1,0:T(8,128)}) async-done(((f32[256,256]{0,1:T(8,128)}, f32[256,256]{1,0:T(8,128)}), (f32[256,256]{0,1:T(8,128)}, f32[256,256]{1,0:T(8,128)})) %all-reduce.4.cloned.1.call-update) | async-done | bytes 524304 | tf_op jit(solution)/shard_map/psum | solution.py:68
  619.9 1.8 copy.30
  621.7 1.7 copy.39
  (15 shorter events, 0.1 us)
Async XLA Ops:
  7.2 28.4 %copy-start = (f32[256,256]{1,0:T(8,128)S(1)}, f32[256,256]{1,0:T(8,128)}, u32[]{:S(2)}) copy-start(f32[256,256]{1,0:T(8,128)} %param.14) | copy-start | bytes 786436
  7.2 338.9 %all-gather.2.cloned.1.call-start = ((), (), s32[]{:S(2)}) async-start(), calls=%async_computation.1 | async-start | bytes 16908288 | tf_op jit(solution)/shard_map/all_gather | solution.py:32
  10.4 5.7 copy-start.10
  17.4 33.8 %all-to-all-start = ((f32[128,8,256]{2,1,0:T(8,128)}), f32[128,8,256]{2,1,0:T(8,128)S(1)}, u32[]{:S(2)}, u32[]{:S(2)}) async-start(f32[128,8,256]{2,1,0:T(8,128)} %bitcast_select_fusion), calls=%async_computation | async-start | bytes 2097152 | tf_op jit(solution)/shard_map/all_to_all | solution.py:37
  28.9 591.0 %all-reduce.4.cloned.1.call-start = ((), (), s32[]{:S(2)}) async-start(), calls=%async_computation.2 | async-start | bytes 1048576 | tf_op jit(solution)/shard_map/psum | solution.py:68
  29.6 5.7 copy-start.7
  29.6 5.9 copy-start.11
  445.0 2.5 copy-start.4
  445.0 2.5 copy-start.5
  445.0 2.5 copy-start.8
  447.5 3.5 copy-start.9
  450.9 4.5 copy-start.3
  450.9 4.5 copy-start.6
  457.9 7.5 %copy-start.2 = (f32[4096,256]{1,0:T(8,128)S(1)}, f32[4096,256]{1,0:T(8,128)}, u32[]{:S(2)}) copy-start(f32[4096,256]{1,0:T(8,128)} %param.13) | copy-start | bytes 12582916
  473.1 150.3 %copy-start.1 = (f32[256,256]{1,0:T(8,128)S(1)}, f32[256,256]{1,0:T(8,128)}, u32[]{:S(2)}) copy-start(f32[256,256]{1,0:T(8,128)} %param.14) | copy-start | bytes 786436
Sparse Core Ops, SparseCore 0:
  10.3 335.7 all-gather.1
  473.2 146.6 all-reduce.3
where the time goes:
time: 636 us; the launch traced here: 630 us
  waiting for transfers between devices  377 us (59%)
  matrix products  83.9 us (13%)
  blocking collectives  67.7 us (11%)
  local copies, waits for them, and re-layouts  48.4 us (8%)
  other arithmetic  26 us (4%)
  between operations  15.9 us (2%)
  starting transfers between devices  11.6 us (2%)
    all_gather x1, waiting for transfers between devices, on_device(): hub_blocks = lax.all_gather(hub_local, ('vert', 'row'), axis=0, tiled=True)  295 us
    psum x1, waiting for transfers between devices, on_device(): lax.psum((local_self, local_neigh, local_bias, local_head), ('vert', 'row'))  74 us
    psum x1, blocking collectives, on_device(): lax.psum((local_self, local_neigh, local_bias, local_head), ('vert', 'row'))  67.7 us
    dot_general x1, matrix products, on_device(): jnp.einsum('tij,tjf->tif', tile_weights, picked, precision=FULL_PRECISION)  34.3 us
    dot_general x1, local copies, waits for them, and re-layouts, on_device(): jnp.einsum('tij,tjf->tif', tile_weights, picked, precision=FULL_PRECISION)  17.7 us
    gather x1, local copies, waits for them, and re-layouts, on_device(): picked = source_table[tile_src]  17.3 us
    concatenate x1, other arithmetic, on_device(): jnp.concatenate([own_blocks, incoming.reshape(-1, tile_size, feature_widt...  15.9 us
    dot_general x1, matrix products, on_device(): jnp.einsum('bt,tif->bif', selector, contrib, precision=FULL_PRECISION)  13.7 us
  transfers between devices with their start and end apart: 3, of which 3 were waited for; matrix products, arithmetic and copies ran while one was open for 4% of the time, Pallas kernels for 0%

commit v1 on v0

--- a/solution.py
+++ b/solution.py
@@ -1,3 +1,4 @@
+import functools
 import math
 import jax
 import jax.numpy as jnp
@@ -5,6 +6,16 @@
 from jax.sharding import PartitionSpec as P
 
 FULL_PRECISION = lax.Precision.HIGHEST
+
+
+def link_strings_now(inner_x, group_axis):
+    found_now = jnp.stack([inner_x for _ in range(lax.axis_size(group_axis))])
+    f_now = lax.all_to_all(found_now, group_axis, 0, 0)
+    t_next = jnp.concatenate(f_now, axis=0)
+    return t_next
+
+
+unite_the_arrays = functools.partial(link_strings_now, group_axis=("vert", "row"))
 
 
 def on_device(
@@ -29,7 +40,7 @@
     slot_count = send_rows.shape[2]
     own_blocks = features.reshape(block_count, tile_size, feature_width)
     hub_local = lax.dynamic_slice_in_dim(own_blocks, hub_block[0], 1, 0)
-    hub_blocks = lax.all_gather(hub_local, ("vert", "row"), axis=0, tiled=True)
+    hub_blocks = unite_the_arrays(hub_local)
     outgoing = features[send_rows[0]]
     slot_index = jnp.arange(slot_count, dtype=jnp.int32)
     alive = slot_index[None, :] < send_count[0][:, None]

time: 636 us -> 579 us (0.910)
  waiting for transfers between devices: 377 us -> 301 us
  local copies, waits for them, and re-layouts: 48.4 us -> 55.6 us
    all_gather x1 -> x0, waiting for transfers between devices: 295 us -> none  [on_device(): hub_blocks = lax.all_gather(hub_local, ('vert', 'row'), axis=0, tiled=True)]
    all_to_all x0 -> x1, waiting for transfers between devices: none -> 207 us  [link_strings_now(): f_now = lax.all_to_all(found_now, group_axis, 0, 0)]
    all_to_all x1, waiting for transfers between devices: 8.03 us -> 18.1 us  [on_device(): lax.all_to_all(outgoing, ('vert', 'row'), split_axis=0, concat_axis=0, ti...]
    another operation x0 -> x1, local copies, waits for them, and re-layouts: none -> 7.83 us  [link_strings_now(): found_now = jnp.stack([inner_x for _ in range(lax.axis_size(group_axis))])]
  transfers between devices with their start and end apart: 3 -> 3, of which waited for: 3 -> 3; matrix products, arithmetic and copies ran while one was open for 4% -> 3% of each run, Pallas kernels for 0% -> 0%
where the time goes in v1:
time: 579 us; the launch traced here: 571 us
  waiting for transfers between devices  301 us (52%)
  matrix products  83.9 us (14%)
  blocking collectives  71.5 us (12%)
  local copies, waits for them, and re-layouts  55.6 us (10%)
  other arithmetic  26.8 us (5%)
  starting transfers between devices  16.5 us (3%)
  between operations  15.8 us (3%)
    all_to_all x1, waiting for transfers between devices, link_strings_now(): f_now = lax.all_to_all(found_now, group_axis, 0, 0)  207 us
    psum x1, waiting for transfers between devices, on_device(): lax.psum((local_self, local_neigh, local_bias, local_head), ('vert', 'row'))  76.1 us
    psum x1, blocking collectives, on_device(): lax.psum((local_self, local_neigh, local_bias, local_head), ('vert', 'row'))  71.5 us
    dot_general x1, matrix products, on_device(): jnp.einsum('tij,tjf->tif', tile_weights, picked, precision=FULL_PRECISION)  34.3 us
    all_to_all x1, waiting for transfers between devices, on_device(): lax.all_to_all(outgoing, ('vert', 'row'), split_axis=0, concat_axis=0, ti...  18.1 us
    dot_general x1, local copies, waits for them, and re-layouts, on_device(): jnp.einsum('tij,tjf->tif', tile_weights, picked, precision=FULL_PRECISION)  17.7 us
    gather x1, local copies, waits for them, and re-layouts, on_device(): picked = source_table[tile_src]  17.3 us
    concatenate x1, other arithmetic, on_device(): jnp.concatenate([own_blocks, incoming.reshape(-1, tile_size, feature_widt...  16.1 us
  transfers between devices with their start and end apart: 3, of which 3 were waited for; matrix products, arithmetic and copies ran while one was open for 3% of the time, Pallas kernels for 0%

profile of v1, /device:TPU:1, one launch (start us, length us, event | category | flops | bytes accessed | tf_op | source)
XLA Modules:
  0.0 571.5 jit_solution(11468503422854393280)
XLA Ops:
  7.2 0.0 copy-start
  7.2 0.7 compare_select_fusion
  7.9 0.1 copy.20
  8.0 0.1 reshape.90
  8.1 0.7 iota_compare_fusion
  8.9 5.7 gather_fusion
  14.5 1.2 bitcast_select_fusion
  15.7 11.5 %all-to-all-start = ((f32[128,8,256]{2,1,0:T(8,128)}), f32[128,8,256]{2,1,0:T(8,128)S(1)}, u32[]{:S(2)}, u32[]{:S(2)}) async-start(f32[128,8,256]{2,1,0:T(8,128)} %bitcast_select_fusion), calls=%async_computation | async-start | bytes 2097152 | tf_op jit(solution)/shard_map/all_to_all | solution.py:48
  27.9 0.9 dynamic-slice_bitcast_fusion
  28.8 18.1 %all-to-all-done = f32[128,8,256]{2,1,0:T(8,128)S(1)} async-done(((f32[128,8,256]{2,1,0:T(8,128)}), f32[128,8,256]{2,1,0:T(8,128)S(1)}, u32[]{:S(2)}, u32[]{:S(2)}) %all-to-all-start) | async-done | bytes 1048608 | tf_op jit(solution)/shard_map/all_to_all | solution.py:48
  46.9 7.8 %stack.2 = f32[128,1,128,256]{3,2,1,0:T(8,128)} broadcast(f32[128,256]{1,0:T(8,128)S(1)} %dynamic-slice_bitcast_fusion), dimensions={2,3} | broadcast | bytes 16908288 | tf_op jit(solution)/shard_map/stack | solution.py:12
  54.7 5.0 all-to-all-start.1
  59.8 0.0 all-reduce.4.cloned.1.call-start
  60.5 0.0 copy-start.7
  60.5 0.0 copy-start.10
  60.5 5.6 reduce_sum.18
  66.1 0.0 copy-done.7
  66.1 0.1 convolution_add_fusion.1
  66.3 0.1 copy.22
  66.4 0.0 copy-done.10
  66.4 0.0 copy-done
  66.4 7.6 %fusion.25 = f32[4096,256]{1,0:T(8,128)} fusion(f32[4096,256]{1,0:T(8,128)} %param.13, f32[256,256]{1,0:T(8,128)S(1)} %copy-done), kind=kOutput, calls=%fused_computation.42 | convolution fusion | flops 3221225472 | bytes 8650752 | tf_op jit(solution)/shard_map/dot_general | solution.py:63
  74.0 206.9 %all-to-all-done.1 = f32[128,1,128,256]{3,2,1,0:T(8,128)} async-done(((f32[128,1,128,256]{3,2,1,0:T(8,128)}), f32[128,1,128,256]{3,2,1,0:T(8,128)}, u32[]{:S(2)}, u32[]{:S(2)}) %all-to-all-start.1) | async-done | bytes 16777248 | tf_op jit(solution)/shard_map/all_to_all | solution.py:13
  280.9 16.1 %pad_maximum_fusion = f32[168,128,256]{2,1,0:T(8,128)} fusion(f32[128,128,256]{2,1,0:T(8,128)} %bitcast.9, f32[8,128,256]{2,1,0:T(8,128)S(1)} %bitcast.63, f32[32,128,256]{2,1,0:T(8,128)} %bitcast.59), kind=kLoop, calls=%fused_computation.2 | loop fusion | flops 11010048 | bytes 44040192 | tf_op jit(solution)/shard_map/concatenate | solution.py:49
  297.0 17.3 %gather_fusion.1 = f32[128,128,256]{2,1,0:T(8,128)} fusion(f32[168,128,256]{2,1,0:T(8,128)} %pad_maximum_fusion, s32[1024]{0:T(1024)S(1)} %pad_clamp_fusion), kind=kCustom, calls=%fused_computation.1 | custom fusion | bytes 33554944 | tf_op jit(solution)/shard_map/gather | solution.py:53
  314.3 34.3 %fusion.26 = f32[128,256,128]{2,1,0:T(8,128)} fusion(f32[128,128,256]{2,1,0:T(8,128)} %gather_fusion.1, f32[128,128,128]{2,1,0:T(8,128)} %param.18), kind=kOutput, calls=%fused_computation.43 | convolution fusion | flops 6442450944 | bytes 41943040 | tf_op jit(solution)/shard_map/tij,tjf->tif/dot_general | solution.py:54
  348.6 17.7 %copy.25 = f32[128,256,128]{1,0,2:T(8,128)} copy(f32[128,256,128]{2,1,0:T(8,128)} %fusion.26) | data formatting | bytes 33554432 | tf_op jit(solution)/shard_map/tij,tjf->tif/dot_general | solution.py:54
  366.3 13.7 %fusion.6 = f32[32,128,256]{2,0,1:T(8,128)S(1)} fusion(f32[32,128,256]{2,1,0:T(8,128)} %bitcast.60, f32[32,128]{0,1:T(8,128)S(1)} %copy.22, f32[128,256,128]{1,0,2:T(8,128)} %copy.25, s32[128]{0:T(128)S(1)} %copy-done.7, pred[128]{0:T(512)(128)(4,1)S(1)} %iota_compare_fusion.2), kind=kOutput, calls=%fused_computation.13 | convolution fusion | flops 1612718080 | bytes 25182848 | tf_op jit(solution)/shard_map/bt,tif->bif/dot_general | solution.py:57
  380.1 0.0 copy-start.5
  380.1 0.0 copy-start.8
  380.1 2.4 copy.23
  382.5 0.0 copy-start.9
  382.6 3.4 fusion.2
  386.0 0.0 copy-start.3
  386.0 0.0 copy-done.9
  386.0 0.0 copy-start.6
  386.0 4.4 fusion.7
  390.5 2.4 fusion.24
  393.0 0.0 copy-start.2
  393.0 7.5 %fusion.27 = f32[256,256]{1,0:T(8,128)} fusion(f32[4096,256]{1,0:T(8,128)S(1)} %bitcast.62, f32[4096,256]{1,0:T(8,128)S(1)} %get-tuple-element.17), kind=kOutput, calls=%fused_computation.44 | convolution fusion | flops 3221225472 | bytes 8650752 | tf_op jit(solution)/shard_map/dot_general | solution.py:76
  400.4 7.7 %convolution_bitcast_fusion = f32[256,256]{0,1:T(8,128)} fusion(f32[4096,256]{1,0:T(8,128)S(1)} %get-tuple-element.17, f32[4096,256]{1,0:T(8,128)S(1)} %copy-done.2), kind=kOutput, calls=%fused_computation.21 | convolution fusion | flops 3221225472 | bytes 8650752 | tf_op jit(solution)/shard_map/dot_general | solution.py:75
  408.1 0.0 all-reduce.4.cloned.1.call-update
  408.1 0.0 copy-start.1
  408.1 5.2 fusion.9
  413.3 71.5 %all-reduce = (f32[256]{0:T(256)}, f32[256]{0:T(256)}) all-reduce(f32[256]{0:T(256)S(1)} %get-tuple-element.16, f32[256]{0:T(256)S(1)} %bitcast.67), channel_id=1, replica_groups=mesh['vert'=64,'row'=2] {'vert','row'}, use_global_device_ids=true, to_apply=%region_4.5 | all-reduce | flops 512 | bytes 4096 | tf_op jit(solution)/shard_map/psum | solution.py:79
  484.8 76.1 %all-reduce.4.cloned.1.call-done = (f32[256,256]{0,1:T(8,128)}, f32[256,256]{1,0:T(8,128)}) async-done(((f32[256,256]{0,1:T(8,128)}, f32[256,256]{1,0:T(8,128)}), (f32[256,256]{0,1:T(8,128)}, f32[256,256]{1,0:T(8,128)})) %all-reduce.4.cloned.1.call-update) | async-done | bytes 524304 | tf_op jit(solution)/shard_map/psum | solution.py:79
  560.9 1.8 copy.24
  562.7 1.7 copy.33
  (13 shorter events, 0.1 us)
Async XLA Ops:
  7.2 59.3 %copy-start = (f32[256,256]{1,0:T(8,128)S(1)}, f32[256,256]{1,0:T(8,128)}, u32[]{:S(2)}) copy-start(f32[256,256]{1,0:T(8,128)} %param.14) | copy-start | bytes 786436
  15.7 31.2 %all-to-all-start = ((f32[128,8,256]{2,1,0:T(8,128)}), f32[128,8,256]{2,1,0:T(8,128)S(1)}, u32[]{:S(2)}, u32[]{:S(2)}) async-start(f32[128,8,256]{2,1,0:T(8,128)} %bitcast_select_fusion), calls=%async_computation | async-start | bytes 2097152 | tf_op jit(solution)/shard_map/all_to_all | solution.py:48
  54.7 226.2 %all-to-all-start.1 = ((f32[128,1,128,256]{3,2,1,0:T(8,128)}), f32[128,1,128,256]{3,2,1,0:T(8,128)}, u32[]{:S(2)}, u32[]{:S(2)}) async-start(f32[128,1,128,256]{3,2,1,0:T(8,128)} %stack.2), calls=%async_computation.1 | async-start | bytes 33554432 | tf_op jit(solution)/shard_map/all_to_all | solution.py:13
  59.8 501.2 %all-reduce.4.cloned.1.call-start = ((), (), s32[]{:S(2)}) async-start(), calls=%async_computation.2 | async-start | bytes 1048576 | tf_op jit(solution)/shard_map/psum | solution.py:79
  60.5 5.7 copy-start.7
  60.5 5.9 %copy-start.10 = (s32[128]{0:T(128)S(1)}, s32[128]{0:T(128)}, u32[]{:S(2)}) copy-start(s32[128]{0:T(128)} %param.20) | copy-start | bytes 1540
  380.0 2.5 copy-start.4
  380.1 2.5 copy-start.5
  380.1 2.5 copy-start.8
  382.5 3.5 copy-start.9
  386.0 4.5 copy-start.3
  386.0 4.5 copy-start.6
  393.0 7.5 %copy-start.2 = (f32[4096,256]{1,0:T(8,128)S(1)}, f32[4096,256]{1,0:T(8,128)}, u32[]{:S(2)}) copy-start(f32[4096,256]{1,0:T(8,128)} %param.13) | copy-start | bytes 12582916
  408.1 156.3 %copy-start.1 = (f32[256,256]{1,0:T(8,128)S(1)}, f32[256,256]{1,0:T(8,128)}, u32[]{:S(2)}) copy-start(f32[256,256]{1,0:T(8,128)} %param.14) | copy-start | bytes 786436
Sparse Core Ops, SparseCore 0:
  408.3 152.6 all-reduce.3
